TPU v7x, 256 devices: a whole 4x4x8 slice. The times are simulated.
256 devices in a mesh: row: 16 (over z, core), col: 4 (over x), seed: 4 (over y).
Axes of the slice: x: 4, y: 4, z: 8, core: 2. Of those that a mesh axis runs over, the one named last changes fastest.
Arguments:
- tiles: bfloat16 [16, 4, 384, 128, 128], P('row', 'col'), may hold values from -0.0390625 to 0.0390625
- tile_out: int32 [16, 4, 384], P('row', 'col'), may hold values from 0 to 15, as said below
- tile_in: int32 [16, 4, 384], P('row', 'col'), may hold values from 0 to 3
- tile_count: int32 [16, 4], P('row', 'col'), may hold values from 1 to 384, as said below
- out_degree: int32 [8192], P(('row', 'col')), may hold values from 1 to 8
- seed_ids: int32 [512, 16], P('seed'), may hold values from 0 to 8191
- prior: float32 [512, 8192], P('seed', ('row', 'col')), may hold values from -6 to 6
Outputs:
- risk: float32 [512, 8192], P('seed', ('row', 'col'))
Inputs may be any that keep to these rules, and one draw needn't show every extreme that they name: `tile_count`: occupied slots of a device come first; some device has all 384 occupied in every draw. `tile_out`: on every device the output blocks named by the occupied slots never fall from one slot to the next; several occupied slots of one device may name the same output block, and the same pair of blocks.
All inputs are finite; a program needn't handle non-finite values.
Results may differ from a plain program's by a relative error of at most 0.0041.
Values may be sent and summed in bfloat16 or wider, within the bound.
A program may use at most 64 MiB of HBM per device.

v0:
```python
import math
import jax
import jax.numpy as jnp
from jax import lax
from jax.sharding import PartitionSpec as P

ITERATIONS = 2
damping = 0.85


def products(blocks, tiles_here, out_ids, in_ids, first_slot, end_slot, base_block, block_total):
    slot_total = tiles_here.shape[0]
    group_size = math.gcd(slot_total, 32)
    sets_here = blocks.shape[1]
    block_edge = tiles_here.shape[2]
    offsets = jnp.arange(group_size, dtype=jnp.int32)
    first_group = first_slot // group_size
    end_group = (end_slot + group_size - 1) // group_size

    def advance(group_index, panel_sum):
        slot_start = group_index * group_size
        tile_block = lax.dynamic_slice_in_dim(tiles_here, slot_start, group_size, 0)
        targets = lax.dynamic_slice_in_dim(out_ids, slot_start, group_size, 0) - base_block
        sources = lax.dynamic_slice_in_dim(in_ids, slot_start, group_size, 0)
        gathered = jnp.take(blocks, sources, axis=0)
        product = jnp.einsum(
            "gsk,gkj->gsj", gathered, tile_block, preferred_element_type=jnp.float32
        )
        slot_here = slot_start + offsets
        valid_mask = ((slot_here >= first_slot) & (slot_here < end_slot)).astype(jnp.float32)
        targets = jnp.clip(targets, 0, block_total - 1)
        return panel_sum.at[targets].add(product * valid_mask[:, None, None])

    zero_panel = jnp.zeros((block_total, sets_here, block_edge), jnp.float32)
    return lax.fori_loop(first_group, end_group, advance, zero_panel)


def local(tiles, tile_out, tile_in, tile_count, out_degree, seed_ids, prior):
    tiles_here = tiles[0, 0]
    out_ids = tile_out[0, 0]
    in_ids = tile_in[0, 0]
    occupied = tile_count[0, 0]
    row_devices = lax.axis_size("row")
    col_devices = lax.axis_size("col")
    sets_here, owned_count = prior.shape
    block_edge = tiles_here.shape[1]
    owned_blocks = owned_count // block_edge
    out_blocks = row_devices * owned_blocks
    own_start = (lax.axis_index("row") * col_devices + lax.axis_index("col")) * owned_count
    local_ids = seed_ids - own_start
    positions = jnp.arange(owned_count, dtype=jnp.int32)
    restart_rows = jnp.sum(
        (local_ids[:, :, None] == positions[None, None, :]).astype(jnp.float32), axis=1
    )
    restart = restart_rows.reshape(sets_here, owned_blocks, block_edge).transpose(1, 0, 2)
    degree = out_degree.astype(jnp.float32).reshape(owned_blocks, 1, block_edge)
    risk_now = prior.reshape(sets_here, owned_blocks, block_edge).transpose(1, 0, 2)
    for round_index in range(ITERATIONS):
        scaled = (risk_now / degree).astype(jnp.bfloat16)
        blocks = lax.all_gather(scaled, "col", axis=0, tiled=True)
        partial_value = products(blocks, tiles_here, out_ids, in_ids, 0, occupied, 0, out_blocks)
        incoming = lax.psum_scatter(partial_value, "row", scatter_dimension=0, tiled=True)
        risk_now = (1.0 - damping) * restart + damping * incoming
    return risk_now.transpose(1, 0, 2).reshape(sets_here, owned_count)


def solution(mesh):
    placed = (
        P("row", "col", None, None, None),
        P("row", "col", None),
        P("row", "col", None),
        P("row", "col"),
        P(("row", "col")),
        P("seed", None),
        P("seed", ("row", "col")),
    )
    return jax.shard_map(
        local, mesh=mesh, in_specs=placed, out_specs=P("seed", ("row", "col")), check_vma=False
    )
```

profile of v0, /device:TPU:4, one launch (start us, length us, event | category | flops | bytes accessed | tf_op | source)
XLA Modules:
  0.0 331.0 jit_solution(5670135569856032543)
XLA Ops:
  7.9 0.8 divide_convert_fusion
  8.7 12.1 %all-gather = bf16[512,128]{1,0:T(8,128)(2,1)S(1)} all-gather(bf16[128,128]{1,0:T(8,128)(2,1)S(1)} %divide_convert_fusion), channel_id=2, replica_groups=mesh['row'=16,'col'=4,'seed'=4] {'col'}, dimensions={0}, use_global_device_ids=true | all-gather | bytes 163840 | tf_op jit(solution)/shard_map/all_gather | solution.py:60
  22.4 21.6 %while.22 = (s32[]{:T(128)}, f32[16,128,128]{2,1,0:T(8,128)S(1)}, s32[]{:T(128)}, s32[384]{0:T(512)S(1)}, s32[384]{0:T(512)S(1)}, /*index=5*/bf16[4,128,128]{2,1...) while((s32[]{:T(128)}, f32[16,128,128]{2,1,0:T(8,128)S(1)}, ...), condition=%wide.region_3.5_spmd.clone, body=%wide.region_1.4_spmd.clone.sunk | while | flops 135792096 | bytes 12588407 | solution.py:35
  22.4 0.7 compare_and_fusion.4
  23.1 1.7 gather_fusion
  24.8 2.0 convolution_multiply_fusion.4
  26.9 2.7 scatter_fusion
  29.6 0.7 compare_and_fusion.4
  30.4 1.7 gather_fusion
  32.0 2.0 convolution_multiply_fusion.4
  34.1 2.7 scatter_fusion
  36.8 0.7 compare_and_fusion.4
  37.6 1.7 gather_fusion
  39.2 2.0 convolution_multiply_fusion.4
  41.4 2.7 scatter_fusion
  44.0 1.0 copy-done.1
  45.6 123.5 %reduce-scatter.3.cloned.1.call-done = f32[1,128,128]{2,1,0:T(8,128)} async-done(((f32[16,128,128]{2,1,0:T(8,128)}), f32[1,128,128]{2,1,0:T(8,128)}) %reduce-scatter.3.cloned.1.call-update) | async-done | bytes 65552 | tf_op jit(solution)/shard_map/reduce_scatter | solution.py:62
  169.1 0.9 fusion.17
  169.9 10.8 %all_gather.7 = bf16[4,128,128]{2,1,0:T(8,128)(2,1)S(1)} all-gather(bf16[1,128,128]{2,1,0:T(8,128)(2,1)S(1)} %fusion.17), channel_id=1, replica_groups=mesh['row'=16,'col'=4,'seed'=4] {'col'}, dimensions={0}, use_global_device_ids=true | all-gather | bytes 163840 | tf_op jit(solution)/shard_map/all_gather | solution.py:60
  180.8 21.6 %while.23 = (s32[]{:T(128)}, f32[16,128,128]{2,1,0:T(8,128)S(1)}, s32[]{:T(128)}, s32[384]{0:T(512)S(1)}, s32[384]{0:T(512)S(1)}, /*index=5*/bf16[4,128,128]{2,1...) while((s32[]{:T(128)}, f32[16,128,128]{2,1,0:T(8,128)S(1)}, ...), condition=%wide.region_7.9_spmd.clone, body=%wide.region_5.8_spmd.clone.sunk | while | flops 135792096 | bytes 12588407 | solution.py:35
  181.6 1.7 gather_fusion.1
  183.3 2.0 convolution_multiply_fusion.5
  185.4 2.7 scatter_fusion.1
  188.8 1.7 gather_fusion.1
  190.5 2.0 convolution_multiply_fusion.5
  192.6 2.7 scatter_fusion.1
  196.0 1.7 gather_fusion.1
  197.7 2.0 convolution_multiply_fusion.5
  199.8 2.7 scatter_fusion.1
  202.5 1.0 copy-done
  203.5 119.2 %reduce-scatter.5.cloned.1.call-done = f32[1,128,128]{2,1,0:T(8,128)} async-done(((f32[16,128,128]{2,1,0:T(8,128)}), f32[1,128,128]{2,1,0:T(8,128)}) %reduce-scatter.5.cloned.1.call-update) | async-done | bytes 65552 | tf_op jit(solution)/shard_map/reduce_scatter | solution.py:62
  322.7 1.5 fusion.18
  (31 shorter events, 5.5 us)
Async XLA Ops:
  6.5 162.5 %reduce-scatter.3.cloned.1.call-start = ((), (), s32[]{:S(2)}) async-start(), calls=%async_computation.2 | async-start | bytes 1114112 | tf_op jit(solution)/shard_map/reduce_scatter | solution.py:62
  22.4 22.7 %copy-start.2 = (s32[128,16]{0,1:T(8,128)S(1)}, s32[128,16]{0,1:T(8,128)}, u32[]{:S(2)}) copy-start(s32[128,16]{0,1:T(8,128)} %param.18) | copy-start | bytes 24580
  44.0 1.0 copy-start.1
  45.0 277.7 %reduce-scatter.5.cloned.1.call-start = ((), (), s32[]{:S(2)}) async-start(), calls=%async_computation.3 | async-start | bytes 1114112 | tf_op jit(solution)/shard_map/reduce_scatter | solution.py:62
  202.5 1.0 copy-start
Sparse Core Ops, SparseCore 0:
  45.2 123.8 reduce-scatter.2
  203.6 119.0 reduce-scatter.4
where the time goes:
time: 332 us; the launch traced here: 331 us
  waiting for transfers between devices  243 us (73%)
  other arithmetic  26.5 us (8%)
  blocking collectives  22.9 us (7%)
  between operations  14.2 us (4%)
  local copies, waits for them, and re-layouts  12.3 us (4%)
  matrix products  12.2 us (4%)
    reduce_scatter x2, waiting for transfers between devices, local(): lax.psum_scatter(partial_value, 'row', scatter_dimension=0, tiled=True)  243 us
    all_gather x2, blocking collectives, local(): blocks = lax.all_gather(scaled, 'col', axis=0, tiled=True)  22.9 us
    scatter-add x6, other arithmetic, advance(): return panel_sum.at[targets].add(product * valid_mask[:, None, None])  15.9 us
    dot_general x6, matrix products, advance(): jnp.einsum('gsk,gkj->gsj', gathered, tile_block, preferred_element_type=j...  12.2 us
    gather x6, local copies, waits for them, and re-layouts, advance(): gathered = jnp.take(blocks, sources, axis=0)  10 us
  transfers between devices with their start and end apart: 2, of which 2 were waited for; matrix products, arithmetic and copies ran while one was open for 0% of the time, Pallas kernels for 0%

commit v1 on v0

--- a/solution.py
+++ b/solution.py
@@ -57,7 +57,10 @@
     risk_now = prior.reshape(sets_here, owned_blocks, block_edge).transpose(1, 0, 2)
     for round_index in range(ITERATIONS):
         scaled = (risk_now / degree).astype(jnp.bfloat16)
-        blocks = lax.all_gather(scaled, "col", axis=0, tiled=True)
+        size = lax.axis_size("col")
+        pieces = jnp.stack([scaled for _ in range(size)])
+        pieces = lax.all_to_all(pieces, "col", split_axis=0, concat_axis=0)
+        blocks = jnp.concatenate(pieces, axis=0)
         partial_value = products(blocks, tiles_here, out_ids, in_ids, 0, occupied, 0, out_blocks)
         incoming = lax.psum_scatter(partial_value, "row", scatter_dimension=0, tiled=True)
         risk_now = (1.0 - damping) * restart + damping * incoming

time: 332 us -> 327 us (0.985)
  blocking collectives: 22.9 us -> 0 us
  starting transfers between devices: 0.04 us -> 10.3 us
  waiting for transfers between devices: 243 us -> 249 us
    all_gather x2 -> x0, blocking collectives: 22.9 us -> none  [local(): blocks = lax.all_gather(scaled, 'col', axis=0, tiled=True)]
    all_to_all x0 -> x2, starting transfers between devices: none -> 10.3 us  [local(): pieces = lax.all_to_all(pieces, 'col', split_axis=0, concat_axis=0)]
    all_to_all x0 -> x2, waiting for transfers between devices: none -> 4.46 us  [local(): pieces = lax.all_to_all(pieces, 'col', split_axis=0, concat_axis=0)]
  transfers between devices with their start and end apart: 2 -> 4, of which waited for: 2 -> 4; matrix products, arithmetic and copies ran while one was open for 0% -> 1% of each run, Pallas kernels for 0% -> 0%
where the time goes in v1:
time: 327 us; the launch traced here: 326 us
  waiting for transfers between devices  249 us (76%)
  other arithmetic  26.5 us (8%)
  between operations  14.2 us (4%)
  local copies, waits for them, and re-layouts  13.6 us (4%)
  matrix products  12.2 us (4%)
  starting transfers between devices  10.3 us (3%)
    reduce_scatter x2, waiting for transfers between devices, local(): lax.psum_scatter(partial_value, 'row', scatter_dimension=0, tiled=True)  244 us
    scatter-add x6, other arithmetic, advance(): return panel_sum.at[targets].add(product * valid_mask[:, None, None])  15.9 us
    dot_general x6, matrix products, advance(): jnp.einsum('gsk,gkj->gsj', gathered, tile_block, preferred_element_type=j...  12.2 us
    all_to_all x2, starting transfers between devices, local(): pieces = lax.all_to_all(pieces, 'col', split_axis=0, concat_axis=0)  10.3 us
    gather x6, local copies, waits for them, and re-layouts, advance(): gathered = jnp.take(blocks, sources, axis=0)  10 us
  transfers between devices with their start and end apart: 4, of which 4 were waited for; matrix products, arithmetic and copies ran while one was open for 1% of the time, Pallas kernels for 0%

profile of v1, /device:TPU:4, one launch (start us, length us, event | category | flops | bytes accessed | tf_op | source)
XLA Modules:
  0.0 325.9 jit_solution(8475140654988433917)
XLA Ops:
  7.2 0.8 divide_convert_fusion
  8.7 5.5 %all-to-all-start = ((bf16[4,1,128,128]{3,2,1,0:T(8,128)(2,1)}), bf16[4,1,128,128]{3,2,1,0:T(8,128)(2,1)S(1)}, u32[]{:S(2)}, u32[]{:S(2)}) async-start(bf16[4,1,128,128]{3,2,1,0:T(8,128)(2,1)} %stack.4), calls=%async_computation | async-start | bytes 262144 | tf_op jit(solution)/shard_map/all_to_all | solution.py:62
  16.3 1.2 all-to-all-done
  17.6 21.6 %while.22 = (s32[]{:T(128)}, f32[16,128,128]{2,1,0:T(8,128)S(1)}, s32[]{:T(128)}, s32[384]{0:T(512)S(1)}, s32[384]{0:T(512)S(1)}, /*index=5*/bf16[4,128,128]{2,1...) while((s32[]{:T(128)}, f32[16,128,128]{2,1,0:T(8,128)S(1)}, ...), condition=%wide.region_3.5_spmd.clone, body=%wide.region_1.4_spmd.clone.sunk | while | flops 135792096 | bytes 12588407 | solution.py:35
  17.6 0.7 compare_and_fusion.4
  18.4 1.7 gather_fusion
  20.0 2.0 convolution_multiply_fusion.4
  22.1 2.7 scatter_fusion
  25.6 1.7 gather_fusion
  27.2 2.0 convolution_multiply_fusion.4
  29.4 2.7 scatter_fusion
  32.8 1.7 gather_fusion
  34.5 2.0 convolution_multiply_fusion.4
  36.6 2.7 scatter_fusion
  39.3 1.0 copy-done.1
  40.8 124.2 %reduce-scatter.3.cloned.1.call-done = f32[1,128,128]{2,1,0:T(8,128)} async-done(((f32[16,128,128]{2,1,0:T(8,128)}), f32[1,128,128]{2,1,0:T(8,128)}) %reduce-scatter.3.cloned.1.call-update) | async-done | bytes 65552 | tf_op jit(solution)/shard_map/reduce_scatter | solution.py:65
  164.9 0.9 fusion.19
  166.5 4.8 %all-to-all-start.1 = ((bf16[4,1,128,128]{3,2,1,0:T(8,128)(2,1)}), bf16[4,1,128,128]{3,2,1,0:T(8,128)(2,1)S(1)}, u32[]{:S(2)}, u32[]{:S(2)}) async-start(bf16[4,1,128,128]{3,2,1,0:T(8,128)(2,1)} %stack.5), calls=%async_computation.2 | async-start | bytes 262144 | tf_op jit(solution)/shard_map/all_to_all | solution.py:62
  171.3 3.3 %all-to-all-done.1 = bf16[4,1,128,128]{3,2,1,0:T(8,128)(2,1)S(1)} async-done(((bf16[4,1,128,128]{3,2,1,0:T(8,128)(2,1)}), bf16[4,1,128,128]{3,2,1,0:T(8,128)(2,1)S(1)}, u32[]{:S(2)}, u32[]{:S(2)}) %all-to-all-start.1) | async-done | bytes 131104 | tf_op jit(solution)/shard_map/all_to_all | solution.py:62
  174.6 21.6 %while.23 = (s32[]{:T(128)}, f32[16,128,128]{2,1,0:T(8,128)S(1)}, s32[]{:T(128)}, s32[384]{0:T(512)S(1)}, s32[384]{0:T(512)S(1)}, /*index=5*/bf16[4,128,128]{2,1...) while((s32[]{:T(128)}, f32[16,128,128]{2,1,0:T(8,128)S(1)}, ...), condition=%wide.region_7.9_spmd.clone, body=%wide.region_5.8_spmd.clone.sunk | while | flops 135792096 | bytes 12588407 | solution.py:35
  175.4 1.7 gather_fusion.1
  177.1 2.0 convolution_multiply_fusion.5
  179.2 2.7 scatter_fusion.1
  182.6 1.7 gather_fusion.1
  184.3 2.0 convolution_multiply_fusion.5
  186.4 2.7 scatter_fusion.1
  189.8 1.7 gather_fusion.1
  191.5 2.0 convolution_multiply_fusion.5
  193.6 2.7 scatter_fusion.1
  196.3 1.0 copy-done
  197.3 120.2 %reduce-scatter.5.cloned.1.call-done = f32[1,128,128]{2,1,0:T(8,128)} async-done(((f32[16,128,128]{2,1,0:T(8,128)}), f32[1,128,128]{2,1,0:T(8,128)}) %reduce-scatter.5.cloned.1.call-update) | async-done | bytes 65552 | tf_op jit(solution)/shard_map/reduce_scatter | solution.py:65
  317.5 1.5 fusion.18
  (35 shorter events, 8.3 us)
Async XLA Ops:
  8.7 8.8 %all-to-all-start = ((bf16[4,1,128,128]{3,2,1,0:T(8,128)(2,1)}), bf16[4,1,128,128]{3,2,1,0:T(8,128)(2,1)S(1)}, u32[]{:S(2)}, u32[]{:S(2)}) async-start(bf16[4,1,128,128]{3,2,1,0:T(8,128)(2,1)} %stack.4), calls=%async_computation | async-start | bytes 262144 | tf_op jit(solution)/shard_map/all_to_all | solution.py:62
  14.2 150.7 %reduce-scatter.3.cloned.1.call-start = ((), (), s32[]{:S(2)}) async-start(), calls=%async_computation.4 | async-start | bytes 1114112 | tf_op jit(solution)/shard_map/reduce_scatter | solution.py:65
  17.6 22.7 %copy-start.2 = (s32[128,16]{0,1:T(8,128)S(1)}, s32[128,16]{0,1:T(8,128)}, u32[]{:S(2)}) copy-start(s32[128,16]{0,1:T(8,128)} %param.18) | copy-start | bytes 24580
  39.2 1.0 copy-start.1
  166.5 8.1 %all-to-all-start.1 = ((bf16[4,1,128,128]{3,2,1,0:T(8,128)(2,1)}), bf16[4,1,128,128]{3,2,1,0:T(8,128)(2,1)S(1)}, u32[]{:S(2)}, u32[]{:S(2)}) async-start(bf16[4,1,128,128]{3,2,1,0:T(8,128)(2,1)} %stack.5), calls=%async_computation.2 | async-start | bytes 262144 | tf_op jit(solution)/shard_map/all_to_all | solution.py:62
  171.2 146.3 %reduce-scatter.5.cloned.1.call-start = ((), (), s32[]{:S(2)}) async-start(), calls=%async_computation.5 | async-start | bytes 1114112 | tf_op jit(solution)/shard_map/reduce_scatter | solution.py:65
  196.3 1.0 copy-start
Sparse Core Ops, SparseCore 0:
  40.4 124.5 reduce-scatter.2
  197.4 120.0 reduce-scatter.4
